TPU v7x, 32 devices: a whole 2x2x4 slice. The times are simulated.
32 devices in a mesh: groups: 1, mode: 32 (over z, y, x, core).
Axes of the slice: x: 2, y: 2, z: 4, core: 2. Of those that a mesh axis runs over, the one named last changes fastest.
Arguments:
- basis: bfloat16 [384, 16384], P('groups', 'mode')
- slab_region: int32 [128], P(('groups', 'mode')), may hold values from 0 to 8
- coef_index: int32 [9, 6], P('groups'), may hold values from 0 to 8
- coef_table: float32 [8], P('groups'), may hold values from 0.2 to 5
Outputs:
- gram: float32 [21, 384, 384], P(None, ('groups', 'mode'))
All inputs are finite; a program needn't handle non-finite values.
Results may differ from a plain program's by a relative error of at most 0.0005.
The roundings to bfloat16 on the way count: a program that leaves them out, or rounds other values in their place, can miss the bound.
Values may be sent and summed in bfloat16 or wider, within the bound.
A program may use at most 128 MiB of HBM per device.

v0:
```python
import functools

import jax
import jax.numpy as jnp
from jax import lax
from jax.experimental import pallas as pl
from jax.experimental.pallas import tpu as pltpu
from jax.sharding import PartitionSpec as P


def plane_size(devices, share):
    size = 1
    while (
        4 * size * size <= 2 * devices
        and devices % (2 * size) == 0
        and 2 * size * share <= 24 << 20
    ):
        size *= 2
    return size


def slab_weights(slab_region, coef_index, coef_table):
    regions = coef_index.shape[0]
    entries = coef_table.shape[0]
    table_hit = (
        coef_index[:, :, None] == jnp.arange(entries, dtype=jnp.int32)[None, None, :]
    ).astype(jnp.float32)
    kappa = jnp.sum(table_hit * coef_table[None, None, :], axis=2)
    region_hit = (slab_region[:, None] == jnp.arange(regions, dtype=jnp.int32)[None, :]).astype(
        jnp.float32
    )
    return jnp.sum(region_hit[:, :, None] * kappa[None, :, :], axis=1)


def one_action(term, here, before, after, across, opposite, kappa):
    value = here.astype(jnp.float32)
    if term == 0:
        stencil = 2.0 * value - before.astype(jnp.float32) - after.astype(jnp.float32)
    elif term == 1:
        stencil = jnp.dot(here, across, preferred_element_type=jnp.float32)
    elif term == 2:
        stencil = value - before.astype(jnp.float32)
    elif term == 3:
        stencil = value - after.astype(jnp.float32)
    elif term == 4:
        stencil = jnp.dot(here, opposite, preferred_element_type=jnp.float32)
    else:
        stencil = value
    return (kappa * stencil).astype(jnp.bfloat16)


def gram_kernel(terms, inner, outer, own, slabs_dev, total_cells, *refs):
    basis, kap, out = refs[:3]
    field, weights, mine, lhs, act, acc = refs[3:9]
    stages = refs[9 : 9 + terms]
    arrived = refs[9 + terms : 9 + 2 * terms]
    codes = refs[9 + 2 * terms : 9 + 3 * terms]
    scales = refs[9 + 3 * terms : 9 + 4 * terms]
    got_scales = refs[9 + 4 * terms : 9 + 5 * terms]
    lvl, lvl_col, lvl_mid, lvl_row, whole, ss, sr = refs[9 + 5 * terms : 16 + 5 * terms]
    load_sem, gs, gr, ks, kr, hs, hr, zs, zr, cs, cr, rs, rr = refs[16 + 5 * terms :]
    rows, width = field.shape[1], field.shape[2]
    slabs = inner * slabs_dev
    local = outer * own
    me = lax.axis_index("mode")
    plane = me // inner
    column = me % inner

    def row_peer(d):
        return plane * inner + lax.rem(column + d, inner)

    def col_peer(d):
        return lax.rem(plane + d, outer) * inner + column

    def remote(src, dst, send, recv, peer):
        return pltpu.make_async_remote_copy(
            src_ref=src,
            dst_ref=dst,
            send_sem=send,
            recv_sem=recv,
            device_id={"mode": peer},
            device_id_type=pl.DeviceIdType.MESH,
        )

    loads = []
    for s in range(slabs_dev):
        loads.append(
            pltpu.make_async_copy(
                basis.at[:, pl.ds(s * width, width)],
                field.at[1 + column * slabs_dev + s],
                load_sem.at[s],
            )
        )
    loads.append(
        pltpu.make_async_copy(
            kap, weights.at[pl.ds(column * slabs_dev, slabs_dev)], load_sem.at[slabs_dev]
        )
    )
    for copy in loads:
        copy.start()

    barrier = pltpu.get_barrier_semaphore()
    for d in range(1, inner):
        pl.semaphore_signal(
            barrier, inc=1, device_id={"mode": row_peer(d)}, device_id_type=pl.DeviceIdType.MESH
        )
    for d in range(1, outer):
        pl.semaphore_signal(
            barrier, inc=1, device_id={"mode": col_peer(d)}, device_id_type=pl.DeviceIdType.MESH
        )
    pl.semaphore_wait(barrier, inner + outer - 2)
    for copy in loads:
        copy.wait()

    chips = inner // 2
    chip = column // 2
    core = column % 2
    sibling = plane * inner + chip * 2 + 1 - core
    spot = pl.ds(column * slabs_dev, slabs_dev)
    small = [
        remote(weights.at[spot], weights.at[spot], ks.at[d - 1], kr.at[d - 1], row_peer(d))
        for d in range(1, inner)
    ]

    def push(origin, slot, peer):
        span = pl.ds(1 + origin * slabs_dev, slabs_dev)
        return remote(field.at[span], field.at[span], gs.at[slot], gr.at[slot], peer)

    far = [
        push(column, d, plane * inner + lax.rem(chip + d, chips) * 2 + core)
        for d in range(1, chips)
    ]
    gathers = [push(column, 0, sibling)]
    for copy in small + far + gathers:
        copy.start()

    wi = lax.broadcasted_iota(jnp.int32, (width, width), 0)
    wj = lax.broadcasted_iota(jnp.int32, (width, width), 1)
    near = jnp.where((wi == wj + 1) | (wj == wi + 1), 1.0, 0.0)
    same = jnp.where(wi == wj, 1.0, 0.0)
    flip = jnp.where(wi + wj == width - 1, 1.0, 0.0)
    across = (2.0 * same - near).astype(jnp.bfloat16)
    opposite = (same - flip).astype(jnp.bfloat16)
    ri = lax.broadcasted_iota(jnp.int32, (local, rows), 0)
    rj = lax.broadcasted_iota(jnp.int32, (local, rows), 1)
    source = ri + column * own
    for a in range(1, outer):
        source = source + jnp.where(ri >= a * own, inner * own - own, 0)
    select = jnp.where(rj == source, 1.0, 0.0).astype(jnp.bfloat16)
    lvl[...] = jnp.zeros_like(lvl)

    def pick(first, count):
        for s in range(count):
            mine[first + s] = jnp.dot(
                select, field[first + s], preferred_element_type=jnp.float32
            ).astype(jnp.bfloat16)

    def own_actions(b, chosen):
        for term in chosen:
            squares = None
            for s in range(slabs_dev):
                at = b * slabs_dev + s
                value = one_action(
                    term,
                    mine[at + 1],
                    None if term in alone else mine[at],
                    None if term in alone else mine[at + 2],
                    across,
                    opposite,
                    weights[at, term : term + 1, :],
                )
                lhs[b, term * local : (term + 1) * local, s * width : (s + 1) * width] = value
                wide = value.astype(jnp.float32)
                squares = wide * wide if squares is None else squares + wide * wide
            lvl[term : term + 1, :] += jnp.sum(squares, axis=0, keepdims=True)

    alone = (1, 4, 5)
    coupled = tuple(term for term in range(terms) if term not in alone)

    def settle(origin):
        pick(1 + origin * slabs_dev, slabs_dev)
        own_actions(origin, alone)

    for copy in small:
        copy.wait()
    settle(column)
    gathers[0].wait()
    settle(chip * 2 + 1 - core)
    for d, copy in enumerate(far, 1):
        copy.wait_recv()
        origin = lax.rem(chip + chips - d, chips) * 2 + core
        relay = push(origin, chips - 1 + d, sibling)
        relay.start()
        gathers.append(relay)
        settle(origin)
    for copy in far:
        copy.wait_send()
    for copy in gathers[1:]:
        copy.wait()
    halos = [
        remote(field.at[slabs], field.at[0], hs.at[0], hr.at[0], col_peer(1)),
        remote(field.at[1], field.at[slabs + 1], hs.at[1], hr.at[1], col_peer(outer - 1)),
    ]
    for copy in halos:
        copy.start()
    for d in range(1, chips):
        settle(lax.rem(chip + chips - d, chips) * 2 + 1 - core)

    @pl.loop(1, inner - 1)
    def _(b):
        own_actions(b, coupled)

    for copy in halos:
        copy.wait()
    pick(0, 1)
    pick(slabs + 1, 1)
    own_actions(0, coupled)
    own_actions(inner - 1, coupled)

    cols = [
        remote(lvl, lvl_col.at[d - 1], cs.at[d - 1], cr.at[d - 1], col_peer(d))
        for d in range(1, outer)
    ]
    for copy in cols:
        copy.start()

    sends = []
    rowsends = []
    for turn, second in enumerate(reversed(range(terms))):
        deep = (second + 1) * local
        acc[0:deep, :] = jnp.zeros((deep, rows), jnp.float32)

        @pl.loop(0, inner // 2)
        def _(half, second=second, deep=deep):
            for u in range(2):
                for s in range(slabs_dev):
                    at = (half * 2 + u) * slabs_dev + s
                    act[u, :, s * width : (s + 1) * width] = one_action(
                        second,
                        field[at + 1],
                        field[at],
                        field[at + 2],
                        across,
                        opposite,
                        weights[at, second : second + 1, :],
                    )
            sums = [
                lax.dot_general(
                    lhs[half * 2 + u, 0:deep, :],
                    act[u],
                    (((1,), (1,)), ((), ())),
                    preferred_element_type=jnp.float32,
                )
                for u in range(2)
            ]
            acc[0:deep, :] += sums[0] + sums[1]

        for a in range(outer):
            for first in range(second + 1):
                value = acc[first * local + a * own : first * local + (a + 1) * own, :]
                stages[second][a, first * own : (first + 1) * own, :] = value
                peak = jnp.max(jnp.abs(value), axis=0, keepdims=True)
                scale = peak * (1.0 / 32000.0)
                scale = jnp.where(scale > 0.0, scale, 1.0)
                scales[second][a, first : first + 1, :] = scale
                whole[first * own : (first + 1) * own, :] = jnp.round(
                    jnp.clip(value / scale, -32767.0, 32767.0)
                )
            codes[second][a] = (
                whole[0 : (second + 1) * own, :].astype(jnp.int32).astype(jnp.int16)
            )
        for d in range(1, outer):
            n = second * (outer - 1) + d - 1
            scale_copy = remote(
                scales[second].at[lax.rem(plane + d, outer)],
                got_scales[second].at[d - 1],
                ss.at[n],
                sr.at[n],
                col_peer(d),
            )
            scale_copy.start()
            sends.append((second, scale_copy))
            copy = remote(
                codes[second].at[lax.rem(plane + d, outer)],
                arrived[second].at[d - 1],
                zs.at[n],
                zr.at[n],
                col_peer(d),
            )
            copy.start()
            sends.append((second, copy))
        if turn == 0:
            for copy in cols:
                copy.wait()
            mid = lvl[...]
            for d in range(1, outer):
                mid = mid + lvl_col[d - 1]
            lvl_mid[...] = mid
            rowsends = [
                remote(lvl_mid, lvl_row.at[d - 1], rs.at[d - 1], rr.at[d - 1], row_peer(d))
                for d in range(1, inner)
            ]
            for copy in rowsends:
                copy.start()

    for copy in rowsends:
        copy.wait()
    total = lvl_mid[...]
    for d in range(1, inner):
        total = total + lvl_row[d - 1]
    level = jnp.sum(total, axis=1, keepdims=True) / (rows * total_cells) + 1e-06
    for second in reversed(range(terms)):
        for q, copy in sends:
            if q == second:
                copy.wait()
        opened = [
            arrived[second][d - 1].astype(jnp.int32).astype(jnp.float32)
            for d in range(1, outer)
        ]
        for first in range(second + 1):
            part = pl.ds(first * own, own)
            value = stages[second][plane, part, :]
            for d in range(1, outer):
                value = value + (
                    opened[d - 1][first * own : (first + 1) * own, :]
                    * got_scales[second][d - 1, first : first + 1, :]
                )
            factor = 1.0 / (
                total_cells * jnp.sqrt(level[first : first + 1] * level[second : second + 1])
            )
            pair = first * terms - first * (first - 1) // 2 + second - first
            out[pair] = value * factor


def per_device(basis, slab_region, coef_index, coef_table):
    terms = coef_index.shape[1]
    rows, cells_dev = basis.shape
    slabs_dev = slab_region.shape[0]
    width = cells_dev // slabs_dev
    devices = lax.axis_size("mode")
    inner = plane_size(devices, 2 * terms * rows * cells_dev)
    outer = devices // inner
    own = rows // devices
    slabs = slabs_dev * inner
    local = outer * own
    slab_kappa = slab_weights(slab_region, coef_index, coef_table)
    kap = jnp.broadcast_to(
        jnp.pad(slab_kappa, ((0, 0), (0, -terms % 8)))[:, :, None],
        (slabs_dev, terms + -terms % 8, width),
    )
    tall = terms + -terms % 8
    f32, b16 = jnp.float32, jnp.bfloat16
    deep = [(q + 1) * own for q in range(terms)]
    dma = pltpu.SemaphoreType.DMA
    return pl.pallas_call(
        functools.partial(
            gram_kernel, terms, inner, outer, own, slabs_dev, cells_dev * devices
        ),
        out_shape=jax.ShapeDtypeStruct((terms * (terms + 1) // 2, own, rows), f32),
        in_specs=[pl.BlockSpec(memory_space=pl.ANY)] * 2,
        out_specs=pl.BlockSpec(memory_space=pltpu.VMEM),
        scratch_shapes=[
            pltpu.VMEM((slabs + 2, rows, width), b16),
            pltpu.VMEM((slabs, tall, width), f32),
            pltpu.VMEM((slabs + 2, local, width), b16),
            pltpu.VMEM((inner, terms * local, cells_dev), b16),
            pltpu.VMEM((2, rows, cells_dev), b16),
            pltpu.VMEM((terms * local, rows), f32),
        ]
        + [pltpu.VMEM((outer, n, rows), f32) for n in deep]
        + [pltpu.VMEM((outer - 1, n, rows), jnp.int16) for n in deep]
        + [pltpu.VMEM((outer, n, rows), jnp.int16) for n in deep]
        + [pltpu.VMEM((outer, n + 1, rows), f32) for n in range(terms)]
        + [pltpu.VMEM((outer - 1, n + 1, rows), f32) for n in range(terms)]
        + [
            pltpu.VMEM((tall, width), f32),
            pltpu.VMEM((outer - 1, tall, width), f32),
            pltpu.VMEM((tall, width), f32),
            pltpu.VMEM((inner - 1, tall, width), f32),
            pltpu.VMEM((deep[-1], rows), f32),
            dma((terms * (outer - 1),)),
            dma((terms * (outer - 1),)),
            dma((slabs_dev + 1,)),
            dma((inner - 1,)),
            dma((inner - 1,)),
            dma((inner - 1,)),
            dma((inner - 1,)),
            dma((2,)),
            dma((2,)),
            dma((terms * (outer - 1),)),
            dma((terms * (outer - 1),)),
            dma((outer - 1,)),
            dma((outer - 1,)),
            dma((inner - 1,)),
            dma((inner - 1,)),
        ],
        compiler_params=pltpu.CompilerParams(
            collective_id=0, has_side_effects=True, vmem_limit_bytes=48 << 20
        ),
    )(basis, kap)


def solution(mesh):
    return jax.shard_map(
        per_device,
        mesh=mesh,
        in_specs=(P("groups", "mode"), P(("groups", "mode")), P("groups", None), P("groups")),
        out_specs=P(None, ("groups", "mode"), None),
        check_vma=False,
    )
```

profile of v0, /device:TPU:0, one launch (start us, length us, event | category | flops | bytes accessed | tf_op | source)
XLA Modules:
  0.0 64.3 jit_solution(15389119947024823515)
XLA Ops:
  0.0 0.0 copy-start.1
  0.0 0.7 %fusion = f32[4,9]{1,0:T(4,128)S(1)} fusion(s32[4]{0:T(128)} %param.5), kind=kLoop, calls=%fused_computation.4 | loop fusion | flops 72 | bytes 160 | tf_op jit(solution)/shard_map/convert_element_type | solution.py:29
  0.7 0.0 copy-done.1
  0.7 0.8 %select_reduce_fusion = f32[9,6]{0,1:T(8,128)S(1)} fusion(f32[8]{0:T(128)S(1)} %copy-done.1, s32[9,6]{0,1:T(8,128)} %param.6), kind=kLoop, calls=%fused_computation | loop fusion | flops 1242 | bytes 464 | tf_op jit(solution)/shard_map/reduce_sum | solution.py:28
  1.5 0.1 multiply_reduce_fusion
  1.6 0.1 copy.9
  1.7 0.1 broadcast_in_dim.2.refs_1_
  1.8 0.0 copy-start
  1.8 1.0 %copy-done = bf16[384,512]{1,0:T(8,128)(2,1)S(1)} copy-done((bf16[384,512]{1,0:T(8,128)(2,1)S(1)}, bf16[384,512]{1,0:T(8,128)(2,1)}, u32[]{:S(2)}) %copy-start) | copy-done | bytes 393240
  2.8 60.6 %shard_map.46 = f32[21,12,384]{2,1,0:T(8,128)S(1)} custom-call(bf16[384,512]{1,0:T(8,128)(2,1)S(1)} %copy-done, f32[4,8,128]{2,1,0:T(8,128)S(1)} %broadcast_in_dim.2.refs_1_), custom_call_target="tpu_custom_call" | custom-call | tf_op jit(solution)/shard_map/pallas_call | solution.py:355
  63.4 0.9 %copy.8 = f32[21,12,384]{2,0,1:T(8,128)} copy(f32[21,12,384]{2,1,0:T(8,128)S(1)} %shard_map.46) | data formatting | bytes 774144 | tf_op jit(solution)/shard_map/pallas_call | solution.py:355
  (1 shorter events, 0.0 us)
Async XLA Ops:
  0.0 0.7 %copy-start.1 = (f32[8]{0:T(128)S(1)}, f32[8]{0:T(128)}, u32[]{:S(2)}) copy-start(f32[8]{0:T(128)} %param.7) | copy-start | bytes 100
  1.8 1.0 %copy-start = (bf16[384,512]{1,0:T(8,128)(2,1)S(1)}, bf16[384,512]{1,0:T(8,128)(2,1)}, u32[]{:S(2)}) copy-start(bf16[384,512]{1,0:T(8,128)(2,1)} %refs_0_.1) | copy-start | bytes 1179652
where the time goes:
time: 64.5 us; the launch traced here: 64.3 us
  Pallas kernels  60.6 us (94%)
  local copies, waits for them, and re-layouts  2.07 us (3%)
  other arithmetic  1.59 us (2%)
    pallas_call x1, Pallas kernels, per_device(): pl.pallas_call(functools.partial(gram_kernel, terms, inner, outer, own, s...  60.6 us

commit v1 on v0

v1 whole, which is shorter than its diff:
```python
import functools

import jax
import jax.numpy as jnp
from jax import lax
from jax.experimental import pallas as pl
from jax.experimental.pallas import tpu as pltpu
from jax.sharding import PartitionSpec as P

MEMBERS = 4
CHUNK = 3


def near_size(outer):
    size = 1
    while outer % (2 * size) == 0 and 8 * size * size <= outer:
        size *= 2
    return size


def chunk_list(terms):
    chunks = []
    for second in reversed(range(terms)):
        pieces = -(-(second + 1) // CHUNK)
        first = 0
        for piece in range(pieces):
            count = -(-(second + 1 - first) // (pieces - piece))
            chunks.append((second, first, count))
            first += count
    return chunks


def one_action(term, here, before, after, across, opposite, kappa):
    value = here.astype(jnp.float32)
    if term == 0:
        stencil = 2.0 * value - before.astype(jnp.float32) - after.astype(jnp.float32)
    elif term == 1:
        stencil = jnp.dot(here, across, preferred_element_type=jnp.float32)
    elif term == 2:
        stencil = value - before.astype(jnp.float32)
    elif term == 3:
        stencil = value - after.astype(jnp.float32)
    elif term == 4:
        stencil = jnp.dot(here, opposite, preferred_element_type=jnp.float32)
    else:
        stencil = value
    return (kappa * stencil).astype(jnp.bfloat16)


def coded(value, floor=1e-30):
    peak = jnp.maximum(jnp.max(jnp.abs(value), axis=0, keepdims=True), floor)
    return jnp.round(value * (32000.0 / peak)), peak * (1.0 / 32000.0)


def gram_kernel(terms, near, far, own, slabs_dev, total_cells, *refs):
    basis, region, index, table, out = refs[:5]
    chunks = chunk_list(terms)
    count = len(chunks)
    field, weights, mine, pickf, lhs1, lhs2, act1, act2, whole = refs[5:14]
    at = 14
    acc = refs[at : at + terms]
    at += terms
    buffers = []
    for _ in range(9):
        buffers.append(refs[at : at + count])
        at += count
    codes1, got1, scale1, gots1, codes2, got2, scale2, gots2, keep = buffers
    lvl0, lvl1, lvl2, in0, in1, in2 = refs[at : at + 6]
    at += 6
    (load_sem, xs, xr, sib_s, sib_r, rel_s, rel_r, hs, hr, hrel_s, hrel_r, ks, kr) = refs[at : at + 13]
    at += 13
    cs1, cr1, ss1, sr1, cs2, cr2, ss2, sr2, ls0, lr0, ls1, lr1, ls2, lr2 = refs[at:]

    rows, width = field.shape[1], field.shape[2]
    entries = table.shape[0]
    slabs = MEMBERS * slabs_dev
    outer = near * far
    local = outer * own
    share = far * own
    me = lax.axis_index("mode")
    group = me // MEMBERS
    member = me % MEMBERS
    chip = member // 2
    core = member % 2
    a = lax.rem(group, near)
    b = group // near

    sibling = group * MEMBERS + chip * 2 + 1 - core
    partner_member = (1 - chip) * 2 + core
    partner = group * MEMBERS + partner_member

    def member_peer(d):
        return group * MEMBERS + lax.rem(member + d, MEMBERS)

    def near_peer(d):
        return (b * near + lax.rem(a + d, near)) * MEMBERS + member

    def far_peer(d):
        return (lax.rem(b + d, far) * near + a) * MEMBERS + member

    def group_peer(d):
        return lax.rem(group + d, outer) * MEMBERS + member

    def remote(src, dst, send, recv, peer):
        return pltpu.make_async_remote_copy(
            src_ref=src,
            dst_ref=dst,
            send_sem=send,
            recv_sem=recv,
            device_id={"mode": peer},
            device_id_type=pl.DeviceIdType.MESH,
        )

    first_slot = 1 + member * slabs_dev
    loads = [
        pltpu.make_async_copy(
            basis.at[:, pl.ds(s * width, width)], field.at[first_slot + s], load_sem.at[s]
        )
        for s in range(slabs_dev)
    ]
    for copy in loads:
        copy.start()

    barrier = pltpu.get_barrier_semaphore()
    greeted = [member_peer(d) for d in range(1, MEMBERS)]
    greeted += [near_peer(d) for d in range(1, near)]
    greeted += [far_peer(d) for d in range(1, far)]
    greeted += [group_peer(1), group_peer(outer - 1)]
    for peer in greeted:
        pl.semaphore_signal(
            barrier, inc=1, device_id={"mode": peer}, device_id_type=pl.DeviceIdType.MESH
        )
    pl.semaphore_wait(barrier, len(greeted))
    for copy in loads:
        copy.wait()

    def turn(k):
        return k + core * (slabs_dev - 1 - 2 * k)

    across_copies = []
    relays = []
    for k in range(slabs_dev):
        slot = first_slot + turn(k)
        across_copies.append(
            remote(field.at[slot], field.at[slot], xs.at[k], xr.at[k], partner)
        )
        slot = 1 + partner_member * slabs_dev + turn(k)
        relays.append(
            remote(field.at[slot], field.at[slot], rel_s.at[k], rel_r.at[k], sibling)
        )
    span = pl.ds(first_slot, slabs_dev)
    beside = remote(field.at[span], field.at[span], sib_s.at[0], sib_r.at[0], sibling)
    for copy in across_copies:
        copy.start()
    beside.start()
    edge = 1 + core * (slabs - 1)
    beyond = (1 - core) * (slabs + 1)
    halo = remote(
        field.at[edge],
        field.at[beyond],
        hs.at[0],
        hr.at[0],
        lax.rem(group + outer + 2 * core - 1, outer) * MEMBERS + member,
    )
    halo_relay = remote(field.at[beyond], field.at[beyond], hrel_s.at[0], hrel_r.at[0], sibling)

    tall = weights.shape[1]
    row_at = lax.broadcasted_iota(jnp.int32, (tall, width), 0)
    for s in range(slabs_dev):
        where = region[s]
        value = jnp.zeros((tall, width), jnp.float32)
        for term in range(terms):
            entry = index[where, term]
            kappa = jnp.where(entry < entries, table[jnp.minimum(entry, entries - 1)], 0.0)
            value = jnp.where(row_at == term, kappa, value)
        weights[member * slabs_dev + s] = value
    spot = pl.ds(member * slabs_dev, slabs_dev)
    small = [
        remote(weights.at[spot], weights.at[spot], ks.at[d - 1], kr.at[d - 1], member_peer(d))
        for d in range(1, MEMBERS)
    ]
    for copy in small:
        copy.start()

    wi = lax.broadcasted_iota(jnp.int32, (width, width), 0)
    wj = lax.broadcasted_iota(jnp.int32, (width, width), 1)
    beside_one = jnp.where((wi == wj + 1) | (wj == wi + 1), 1.0, 0.0)
    same = jnp.where(wi == wj, 1.0, 0.0)
    flip = jnp.where(wi + wj == width - 1, 1.0, 0.0)
    across = (2.0 * same - beside_one).astype(jnp.bfloat16)
    opposite = (same - flip).astype(jnp.bfloat16)
    ri = lax.broadcasted_iota(jnp.int32, (local, rows), 0)
    rj = lax.broadcasted_iota(jnp.int32, (local, rows), 1)
    source = ri
    for da in range(near):
        for db in range(far):
            place = da * far + db
            home = lax.rem(b + db, far) * near + lax.rem(a + da, near)
            shift = (home * MEMBERS + member) * own - place * own
            source = jnp.where(ri >= place * own, ri + shift, source)
    pickf[...] = jnp.where(rj == source, 1.0, 0.0)
    select = pickf[...].astype(jnp.bfloat16)

    def pick(first, number):
        for s in range(number):
            mine[first + s] = jnp.dot(
                select, field[first + s], preferred_element_type=jnp.float32
            ).astype(jnp.bfloat16)

    def acted(term, source_ref, slab):
        alone = term in (1, 4, 5)
        return one_action(
            term,
            source_ref[slab + 1],
            None if alone else source_ref[slab],
            None if alone else source_ref[slab + 2],
            across,
            opposite,
            weights[slab, term : term + 1, :],
        )

    inner_count = 2 * slabs_dev - 2
    inner_first = 2 + inner_count * chip
    part1 = [inner_first + s for s in range(inner_count)]
    part2 = [chip * (slabs - 2) + s for s in range(2)]
    part2 += [(1 - chip) * 2 * slabs_dev + s for s in range(2 * slabs_dev)]

    def own_actions(lhs, part):
        for term in range(terms):
            for s, slab in enumerate(part):
                lhs[term * local : (term + 1) * local, s * width : (s + 1) * width] = acted(
                    term, mine, slab
                )

    def all_actions(act, part, second):
        for s, slab in enumerate(part):
            act[second % 2, :, s * width : (s + 1) * width] = acted(second, field, slab)

    def product(lhs, act, second):
        return lax.dot_general(
            lhs[0 : (second + 1) * local, :],
            act[second % 2],
            (((1,), (1,)), ((), ())),
            preferred_element_type=jnp.float32,
        )

    across_copies[0].wait_recv()
    relays[0].start()
    halo.start()
    beside.wait()
    for copy in small:
        copy.wait()
    relays[0].wait_recv()
    pick(inner_first, inner_count + 2)
    own_actions(lhs1, part1)
    order = list(reversed(range(terms)))
    for spot_at, second in enumerate(order):
        all_actions(act1, part1, second)
        acc[second][...] = product(lhs1, act1, second)
        if 1 <= spot_at + 1 < slabs_dev:
            across_copies[spot_at + 1].wait_recv()
            relays[spot_at + 1].start()
        if spot_at == 2:
            halo.wait_recv()
            halo_relay.start()
    for copy in relays[1:]:
        copy.wait_recv()
    halo_relay.wait_recv()
    pick(chip * slabs, 2)
    pick((1 - chip) * (2 * slabs_dev + 2), 2 * slabs_dev)
    own_actions(lhs2, part2)

    lvl0[...] = jnp.zeros_like(lvl0)
    sends = []
    stage1 = [[] for _ in chunks]
    for second in order:
        all_actions(act2, part2, second)
        acc[second][...] += product(lhs2, act2, second)
        for n, (chunk_second, first, number) in enumerate(chunks):
            if chunk_second != second:
                continue
            for d in range(1, near):
                for i in range(number):
                    base = (first + i) * local + d * share
                    code, scale = coded(acc[second][base : base + share, :])
                    codes1[n][d - 1, i * share : (i + 1) * share, :] = code.astype(
                        jnp.int32
                    ).astype(jnp.int16)
                    scale1[n][d - 1, i : i + 1, :] = scale
                sem = n * (near - 1) + d - 1
                for src, dst, s_sem, r_sem in (
                    (scale1, gots1, ss1, sr1),
                    (codes1, got1, cs1, cr1),
                ):
                    copy = remote(
                        src[n].at[d - 1],
                        dst[n].at[d - 1],
                        s_sem.at[sem],
                        r_sem.at[sem],
                        near_peer(d),
                    )
                    copy.start()
                    stage1[n].append(copy)
                    sends.append(copy)
        lvl0[second : second + 1, :] = jnp.sum(
            acc[second][second * local : (second + 1) * local, :] * pickf[...],
            axis=0,
            keepdims=True,
        )

    def spread(src, dst, s_sem, r_sem, peer_of, number):
        copies = [
            remote(src, dst.at[d - 1], s_sem.at[d - 1], r_sem.at[d - 1], peer_of(d))
            for d in range(1, number)
        ]
        for copy in copies:
            copy.start()
        return copies

    def gathered(copies, src, dst):
        for copy in copies:
            copy.wait_recv()
        sends.extend(copies)
        total = src[...]
        for n in range(len(copies)):
            total = total + dst[n]
        return total

    level_copies = spread(lvl0, in0, ls0, lr0, near_peer, near)

    stage2 = [[] for _ in chunks]
    for n, (second, first, number) in enumerate(chunks):
        for copy in stage1[n]:
            copy.wait_recv()
        for i in range(number):
            base = (first + i) * local
            value = acc[second][base : base + share, :]
            for d in range(1, near):
                part = got1[n][d - 1, i * share : (i + 1) * share, :]
                value = value + (
                    part.astype(jnp.int32).astype(jnp.float32) * gots1[n][d - 1, i : i + 1, :]
                )
            keep[n][i * own : (i + 1) * own, :] = value[0:own]
            code, scale = coded(value[own:])
            scale2[n][i : i + 1, :] = scale
            for d in range(1, far):
                whole[d - 1, i * own : (i + 1) * own, :] = code[(d - 1) * own : d * own]
        for d in range(1, far):
            codes2[n][d - 1] = (
                whole[d - 1, 0 : number * own, :].astype(jnp.int32).astype(jnp.int16)
            )
            sem = n * (far - 1) + d - 1
            for src, dst, s_sem, r_sem in (
                (scale2[n], gots2, ss2, sr2),
                (codes2[n].at[d - 1], got2, cs2, cr2),
            ):
                copy = remote(src, dst[n].at[d - 1], s_sem.at[sem], r_sem.at[sem], far_peer(d))
                copy.start()
                stage2[n].append(copy)
                sends.append(copy)
        if n == 0:
            lvl1[...] = gathered(level_copies, lvl0, in0)
            level_copies = spread(lvl1, in1, ls1, lr1, far_peer, far)
        if n == count // 2:
            lvl2[...] = gathered(level_copies, lvl1, in1)
            level_copies = spread(lvl2, in2, ls2, lr2, member_peer, MEMBERS)

    total = gathered(level_copies, lvl2, in2)
    level = jnp.sum(total, axis=1, keepdims=True) / (rows * total_cells) + 1e-06
    for n, (second, first, number) in enumerate(chunks):
        for copy in stage2[n]:
            copy.wait_recv()
        opened = [got2[n][d - 1].astype(jnp.int32).astype(jnp.float32) for d in range(1, far)]
        for i in range(number):
            q = first + i
            value = keep[n][i * own : (i + 1) * own, :]
            for d in range(1, far):
                value = value + (
                    opened[d - 1][i * own : (i + 1) * own, :] * gots2[n][d - 1, i : i + 1, :]
                )
            factor = 1.0 / (total_cells * jnp.sqrt(level[q : q + 1] * level[second : second + 1]))
            pair = q * terms - q * (q - 1) // 2 + second - q
            out[pair] = value * factor
    for copy in sends + across_copies + relays + [halo, halo_relay]:
        copy.wait_send()


def per_device(basis, slab_region, coef_index, coef_table):
    terms = coef_index.shape[1]
    rows, cells_dev = basis.shape
    slabs_dev = slab_region.shape[0]
    width = cells_dev // slabs_dev
    devices = lax.axis_size("mode")
    outer = devices // MEMBERS
    near = near_size(outer)
    far = outer // near
    own = rows // devices
    slabs = slabs_dev * MEMBERS
    local = outer * own
    share = far * own
    chunks = chunk_list(terms)
    count = len(chunks)
    tall = terms + -terms % 8
    f32, b16, i16 = jnp.float32, jnp.bfloat16, jnp.int16
    k1 = (2 * slabs_dev - 2) * width
    k2 = (2 * slabs_dev + 2) * width
    dma = pltpu.SemaphoreType.DMA
    vmem = pltpu.VMEM
    most = max(number for _, _, number in chunks)
    scratch = [
        vmem((slabs + 2, rows, width), b16),
        vmem((slabs, tall, width), f32),
        vmem((slabs + 2, local, width), b16),
        vmem((local, rows), f32),
        vmem((terms * local, k1), b16),
        vmem((terms * local, k2), b16),
        vmem((2, rows, k1), b16),
        vmem((2, rows, k2), b16),
        vmem((far - 1, most * own, rows), f32),
    ]
    scratch += [vmem(((q + 1) * local, rows), f32) for q in range(terms)]
    scratch += [vmem((near - 1, n * share, rows), i16) for _, _, n in chunks] * 2
    scratch += [vmem((near - 1, n, rows), f32) for _, _, n in chunks] * 2
    scratch += [vmem((far - 1, n * own, rows), i16) for _, _, n in chunks] * 2
    scratch += [vmem((n, rows), f32) for _, _, n in chunks]
    scratch += [vmem((far - 1, n, rows), f32) for _, _, n in chunks]
    scratch += [vmem((n * own, rows), f32) for _, _, n in chunks]
    scratch += [vmem((tall, rows), f32)] * 3
    scratch += [vmem((n - 1, tall, rows), f32) for n in (near, far, MEMBERS)]
    scratch += [dma((slabs_dev,))] * 3
    scratch += [dma((1,))] * 2
    scratch += [dma((slabs_dev,))] * 2
    scratch += [dma((1,))] * 4
    scratch += [dma((MEMBERS - 1,))] * 2
    scratch += [dma((count * (near - 1),))] * 4
    scratch += [dma((count * (far - 1),))] * 4
    for n in (near, far, MEMBERS):
        scratch += [dma((n - 1,))] * 2
    smem = pl.BlockSpec(memory_space=pltpu.SMEM)
    return pl.pallas_call(
        functools.partial(
            gram_kernel, terms, near, far, own, slabs_dev, cells_dev * devices
        ),
        out_shape=jax.ShapeDtypeStruct((terms * (terms + 1) // 2, own, rows), f32),
        in_specs=[pl.BlockSpec(memory_space=pl.ANY), smem, smem, smem],
        out_specs=pl.BlockSpec(memory_space=pltpu.VMEM),
        scratch_shapes=scratch,
        compiler_params=pltpu.CompilerParams(
            collective_id=0, has_side_effects=True, vmem_limit_bytes=48 << 20
        ),
    )(basis, slab_region, coef_index, coef_table)


def solution(mesh):
    return jax.shard_map(
        per_device,
        mesh=mesh,
        in_specs=(P("groups", "mode"), P(("groups", "mode")), P("groups", None), P("groups")),
        out_specs=P(None, ("groups", "mode"), None),
        check_vma=False,
    )
```

time: 64.5 us -> 66.9 us (1.037)
  Pallas kernels: 60.6 us -> 64 us
  other arithmetic: 1.59 us -> 0 us
    pallas_call x1, Pallas kernels: 60.6 us -> 64 us  [per_device(): pl.pallas_call(functools.partial(gram_kernel, terms, near, far, own, slab...]
    reduce_sum x2 -> x0, other arithmetic: 0.85 us -> none  [the longest x1 0.77 us: slab_weights(): kappa = jnp.sum(table_hit * coef_table[None, None, :], axis=2)]
    convert_element_type x1 -> x0, other arithmetic: 0.74 us -> none  [slab_weights(): (slab_region[:, None] == jnp.arange(regions, dtype=jnp.int32)[None, :]).a...]
    unnamed x5 -> x7, local copies, waits for them, and re-layouts: 1.1 us -> 1.8 us
where the time goes in v1:
time: 66.9 us; the launch traced here: 66.7 us
  Pallas kernels  64 us (96%)
  local copies, waits for them, and re-layouts  2.69 us (4%)
    pallas_call x1, Pallas kernels, per_device(): pl.pallas_call(functools.partial(gram_kernel, terms, near, far, own, slab...  64 us
    unnamed x7, local copies, waits for them, and re-layouts  1.8 us

profile of v1, /device:TPU:0, one launch (start us, length us, event | category | flops | bytes accessed | tf_op | source)
XLA Modules:
  0.0 66.7 jit_solution(2607707643038906436)
XLA Ops:
  0.0 0.0 copy-start.2
  0.0 0.0 copy-start.1
  0.0 0.8 %copy.5.refs_2_ = s32[9,6]{1,0:T(8,128)S(1)} copy(s32[9,6]{0,1:T(8,128)} %param.6) | data formatting | bytes 432 | tf_op args[2]
  0.8 0.0 copy-done.2
  0.8 0.0 copy-done.1
  0.8 0.0 copy-start
  0.8 1.0 %copy-done = bf16[384,512]{1,0:T(8,128)(2,1)S(1)} copy-done((bf16[384,512]{1,0:T(8,128)(2,1)S(1)}, bf16[384,512]{1,0:T(8,128)(2,1)}, u32[]{:S(2)}) %copy-start) | copy-done | bytes 393240
  1.8 64.0 %shard_map.46 = f32[21,12,384]{2,1,0:T(8,128)S(1)} custom-call(bf16[384,512]{1,0:T(8,128)(2,1)S(1)} %copy-done, s32[4]{0:T(128)S(1)} %copy-done.1, s32[9,6]{1,0:T(8,128)S(1)} %copy.5.refs_2_, f32[8]{0:T(128)S(1)} %copy-done.2), custom_call_target="tpu_custom_call" | custom-call | tf_op jit(solution)/shard_map/pallas_call | solution.py:440
  65.8 0.9 %copy.6 = f32[21,12,384]{2,0,1:T(8,128)} copy(f32[21,12,384]{2,1,0:T(8,128)S(1)} %shard_map.46) | data formatting | bytes 774144 | tf_op jit(solution)/shard_map/pallas_call | solution.py:440
Async XLA Ops:
  0.0 0.8 %copy-start.2 = (f32[8]{0:T(128)S(1)}, f32[8]{0:T(128)}, u32[]{:S(2)}) copy-start(f32[8]{0:T(128)} %refs_3_.1) | copy-start | bytes 100
  0.0 0.8 %copy-start.1 = (s32[4]{0:T(128)S(1)}, s32[4]{0:T(128)}, u32[]{:S(2)}) copy-start(s32[4]{0:T(128)} %refs_1_.1) | copy-start | bytes 52
  0.8 1.0 %copy-start = (bf16[384,512]{1,0:T(8,128)(2,1)S(1)}, bf16[384,512]{1,0:T(8,128)(2,1)}, u32[]{:S(2)}) copy-start(bf16[384,512]{1,0:T(8,128)(2,1)} %refs_0_.1) | copy-start | bytes 1179652

commit v2 on v1

v2 whole, which is shorter than its diff:
```python
import functools

import jax
import jax.numpy as jnp
from jax import lax
from jax.experimental import pallas as pl
from jax.experimental.pallas import tpu as pltpu
from jax.sharding import PartitionSpec as P

CHUNK = 2
WINDOW = 4


def chunk_list(terms):
    chunks = []
    for second in reversed(range(terms)):
        first = 0
        while first <= second:
            number = min(CHUNK, second + 1 - first)
            chunks.append((second, first, number))
            first += number
    return chunks


def one_action(term, here, before, after, across, opposite, kappa):
    value = here.astype(jnp.float32)
    if term == 0:
        stencil = 2.0 * value - before.astype(jnp.float32) - after.astype(jnp.float32)
    elif term == 1:
        stencil = jnp.dot(here, across, preferred_element_type=jnp.float32)
    elif term == 2:
        stencil = value - before.astype(jnp.float32)
    elif term == 3:
        stencil = value - after.astype(jnp.float32)
    elif term == 4:
        stencil = jnp.dot(here, opposite, preferred_element_type=jnp.float32)
    else:
        stencil = value
    return (kappa * stencil).astype(jnp.bfloat16)


def coded(value, floor=1e-30):
    peak = jnp.maximum(jnp.max(jnp.abs(value), axis=0, keepdims=True), floor)
    return jnp.round(value * (32000.0 / peak)), peak * (1.0 / 32000.0)


def short(code):
    return code.astype(jnp.int32).astype(jnp.int16)


def wide(code):
    return code.astype(jnp.int32).astype(jnp.float32)


def gram_kernel(terms, highs, own, slabs_dev, total_cells, *refs):
    basis, region, index, table, out = refs[:5]
    chunks = chunk_list(terms)
    count = len(chunks)
    field, packed, weights, mine, lhs1, lhs2, lhs3, act1, act2, act3, whole2, whole3 = refs[5:17]
    at = 17
    acc = refs[at : at + terms]
    at += terms
    buffers = []
    for _ in range(14):
        buffers.append(refs[at : at + count])
        at += count
    (codes1, got1, scale1, gots1, codes2, got2, scale2, gots2) = buffers[:8]
    (codes3, got3, scale3, gots3, mid, keep) = buffers[8:]
    lvl = refs[at : at + 4]
    lvl_in = refs[at + 4 : at + 8]
    at += 8
    (load_sem, xs, xr, sib_s, sib_r, rel_s, rel_r, hs, hr, hrel_s, hrel_r, ks, kr) = refs[at : at + 13]
    at += 13
    (cs1, cr1, ss1, sr1, cs2, cr2, ss2, sr2, cs3, cr3, ss3, sr3) = refs[at : at + 12]
    lvl_s = refs[at + 12 : at + 16]
    lvl_r = refs[at + 16 : at + 20]

    rows, width = field.shape[1], field.shape[2]
    entries = table.shape[0]
    span = 2 * slabs_dev
    stride = span + 2
    chips = 8 * highs
    local = 4 * highs * own
    half = local // 2
    quarter = local // 4
    me = lax.axis_index("mode")
    chip = me // 2
    core = me % 2
    x = chip % 2
    y = (chip // 2) % 2
    level_z = chip // 4
    low = level_z % 2
    high = level_z // 2

    def across_pair(c):
        return c + 4 - 8 * ((c // 4) % 2)

    def device(c):
        return c * 2 + core

    other = across_pair(chip)
    step = 2 * core - 1
    ahead = lax.rem(chip + chips + step, chips)
    behind = lax.rem(chip + chips - step, chips)
    other_ahead = across_pair(lax.rem(other + chips + step, chips))
    other_behind = across_pair(lax.rem(other + chips - step, chips))
    sibling = chip * 2 + 1 - core
    partner = device(other)
    cross = other * 2 + 1 - core
    x_peer = device(chip + 1 - 2 * x)
    y_peer = device(chip + 2 - 4 * y)

    def high_peer(d):
        return device(chip + 8 * (lax.rem(high + d, highs) - high))

    def remote(src, dst, send, recv, peer):
        return pltpu.make_async_remote_copy(
            src_ref=src,
            dst_ref=dst,
            send_sem=send,
            recv_sem=recv,
            device_id={"mode": peer},
            device_id_type=pl.DeviceIdType.MESH,
        )

    first_slot = 1 + core * slabs_dev
    loads = [
        pltpu.make_async_copy(
            basis.at[:, pl.ds(s * width, width)], field.at[first_slot + s], load_sem.at[s]
        )
        for s in range(slabs_dev)
    ]
    for copy in loads:
        copy.start()

    barrier = pltpu.get_barrier_semaphore()
    greeted = [sibling, partner, cross, x_peer, y_peer]
    greeted += [high_peer(d) for d in range(1, highs)]
    greeted += [device(c) for c in (ahead, behind, other_ahead, other_behind)]
    for peer in greeted:
        pl.semaphore_signal(
            barrier, inc=1, device_id={"mode": peer}, device_id_type=pl.DeviceIdType.MESH
        )

    tall = weights.shape[1]
    piece = width // slabs_dev
    row_at = lax.broadcasted_iota(jnp.int32, (tall, width), 0)
    lane_at = lax.broadcasted_iota(jnp.int32, (tall, width), 1)
    value = jnp.zeros((tall, width), jnp.float32)
    for s in range(slabs_dev):
        where = region[s]
        lanes = (lane_at >= s * piece) & (lane_at < (s + 1) * piece)
        for term in range(terms):
            entry = index[term, where]
            kappa = jnp.where(entry < entries, table[jnp.minimum(entry, entries - 1)], 0.0)
            value = jnp.where(lanes & (row_at == term), kappa, value)
    packed[core] = value

    wi = lax.broadcasted_iota(jnp.int32, (width, width), 0)
    wj = lax.broadcasted_iota(jnp.int32, (width, width), 1)
    beside_one = jnp.where((wi == wj + 1) | (wj == wi + 1), 1.0, 0.0)
    same = jnp.where(wi == wj, 1.0, 0.0)
    flip = jnp.where(wi + wj == width - 1, 1.0, 0.0)
    across = (2.0 * same - beside_one).astype(jnp.bfloat16)
    opposite = (same - flip).astype(jnp.bfloat16)
    ri = lax.broadcasted_iota(jnp.int32, (local, rows), 0)
    rj = lax.broadcasted_iota(jnp.int32, (local, rows), 1)
    source = ri
    for dx in range(2):
        for dy in range(2):
            for dh in range(highs):
                place = (dx * 2 + dy) * highs + dh
                home_z = lax.rem(high + dh, highs) * 2 + low
                home_y = y + dy - 2 * y * dy
                home_x = x + dx - 2 * x * dx
                home = ((home_z * 2 + home_y) * 2 + home_x) * 2 + core
                source = jnp.where(ri >= place * own, ri + (home * own - place * own), source)
    select = jnp.where(rj == source, 1.0, 0.0).astype(jnp.bfloat16)

    pl.semaphore_wait(barrier, len(greeted))
    for copy in loads:
        copy.wait()

    def turn(k):
        return k + core * (slabs_dev - 1 - 2 * k)

    across_copies = []
    relays = []
    for k in range(slabs_dev):
        slot = first_slot + turn(k)
        across_copies.append(
            remote(field.at[slot], field.at[stride + slot], xs.at[k], xr.at[k], partner)
        )
        slot = stride + slot
        relays.append(remote(field.at[slot], field.at[slot], rel_s.at[k], rel_r.at[k], sibling))
    block = pl.ds(first_slot, slabs_dev)
    beside = remote(field.at[block], field.at[block], sib_s.at[0], sib_r.at[0], sibling)
    edge = 1 + core * (span - 1)
    beyond = (1 - core) * (span + 1)
    halos = []
    halo_relays = []
    for n, target in enumerate((ahead, other_ahead)):
        halos.append(
            remote(
                field.at[n * stride + edge],
                field.at[n * stride + beyond],
                hs.at[n],
                hr.at[n],
                device(target),
            )
        )
        slot = n * stride + beyond
        halo_relays.append(
            remote(field.at[slot], field.at[slot], hrel_s.at[n], hrel_r.at[n], sibling)
        )
    small = [
        remote(packed.at[core], packed.at[core + shift], ks.at[n], kr.at[n], peer)
        for n, (peer, shift) in enumerate(((sibling, 0), (partner, 2), (cross, 2)))
    ]
    for copy in small:
        copy.start()
    across_copies[0].start()
    halos[0].start()
    beside.start()
    for copy in across_copies[1:]:
        copy.start()

    def pick(first, number):
        for s in range(number):
            mine[first + s] = jnp.dot(
                select, field[first + s], preferred_element_type=jnp.float32
            ).astype(jnp.bfloat16)

    def acted(term, source_ref, spot):
        part, slab = spot
        alone = term in (1, 4, 5)
        slot = part * stride + 1 + slab
        return one_action(
            term,
            source_ref[slot],
            None if alone else source_ref[slot - 1],
            None if alone else source_ref[slot + 1],
            across,
            opposite,
            weights[part * span + slab, term : term + 1, :],
        )

    lvl[0][...] = jnp.zeros_like(lvl[0])

    def own_actions(lhs, part):
        for term in range(terms):
            squares = None
            for s, spot in enumerate(part):
                value = acted(term, mine, spot)
                lhs[term * local : (term + 1) * local, s * width : (s + 1) * width] = value
                value = value.astype(jnp.float32)
                squares = value * value if squares is None else squares + value * value
            lvl[0][term : term + 1, :] += jnp.sum(squares, axis=0, keepdims=True)

    def all_actions(act, part, second):
        for s, spot in enumerate(part):
            act[second % 2, :, s * width : (s + 1) * width] = acted(second, field, spot)

    def product(lhs, act, second):
        return lax.dot_general(
            lhs[0 : (second + 1) * local, :],
            act[second % 2],
            (((1,), (1,)), ((), ())),
            preferred_element_type=jnp.float32,
        )

    sends = []

    def spread(n, peers):
        copies = [
            remote(lvl[n], lvl_in[n].at[d], lvl_s[n].at[d], lvl_r[n].at[d], peer)
            for d, peer in enumerate(peers)
        ]
        for copy in copies:
            copy.start()
        sends.extend(copies)
        return copies

    def gathered(n, copies):
        for copy in copies:
            copy.wait_recv()
        total = lvl[n][...]
        for d in range(len(copies)):
            total = total + lvl_in[n][d]
        return total

    ends = slabs_dev - 2
    part1 = [(0, s) for s in range(span)]
    part2 = [(1, s) for s in range(span) if s < ends or s >= span - ends]
    part3 = [(1, s) for s in range(ends, span - ends)]
    order = list(reversed(range(terms)))

    halos[0].wait_recv()
    halo_relays[0].start()
    beside.wait()
    for copy in small:
        copy.wait()
    for n in range(4):
        source_value = packed[n]
        for s in range(slabs_dev):
            lanes = (lane_at >= s * piece) & (lane_at < (s + 1) * piece)
            value = jnp.where(lanes, source_value, 0.0)
            shift = piece
            while shift < width:
                value = value + pltpu.roll(value, shift, 1)
                shift *= 2
            weights[n * slabs_dev + s] = value
    across_copies[0].wait_recv()
    relays[0].start()
    halos[1].start()
    halo_relays[0].wait_recv()
    pick(0, stride)
    own_actions(lhs1, part1)
    for n, second in enumerate(order):
        all_actions(act1, part1, second)
        acc[second][...] = product(lhs1, act1, second)
        if n == 0:
            across_copies[1].wait_recv()
            relays[1].start()
        if n == 1:
            halos[1].wait_recv()
            halo_relays[1].start()
        if 2 <= n < slabs_dev - 1 + 0:
            across_copies[n].wait_recv()
            relays[n].start()
    for copy in relays[: slabs_dev - 1] + [halo_relays[1]]:
        copy.wait_recv()
    pick(stride, ends + 2)
    pick(stride + span - ends, ends + 2)
    own_actions(lhs2, part2)
    for n, second in enumerate(order):
        all_actions(act2, part2, second)
        acc[second][...] += product(lhs2, act2, second)
        if n == 2:
            across_copies[slabs_dev - 1].wait_recv()
            relays[slabs_dev - 1].start()
    relays[slabs_dev - 1].wait_recv()
    pick(stride + ends + 2, span - 2 * ends - 2)
    own_actions(lhs3, part3)
    level_copies = spread(0, [x_peer])

    stage1 = []
    stage2 = []
    stage3 = []

    def exchange(n, src, dst, scale, gots, sems, peer):
        cs, cr, ss, sr = sems
        return [
            remote(scale[n], gots[n], ss.at[n], sr.at[n], peer),
            remote(src[n], dst[n], cs.at[n], cr.at[n], peer),
        ]

    for turn_at, second in enumerate(order):
        all_actions(act3, part3, second)
        acc[second][...] += product(lhs3, act3, second)
        if turn_at == 0:
            lvl[1][...] = gathered(0, level_copies)
            level_copies = spread(1, [y_peer])
        if turn_at == 2:
            lvl[2][...] = gathered(1, level_copies)
            level_copies = spread(2, [sibling, partner, cross])
        if turn_at == 4:
            lvl[3][...] = gathered(2, level_copies)
            level_copies = spread(3, [high_peer(d) for d in range(1, highs)])
        for n, (chunk_second, first, number) in enumerate(chunks):
            if chunk_second != second:
                continue
            for i in range(number):
                base = (first + i) * local
                if n % 2 == 0:
                    value = acc[second][base + half : base + local, :]
                else:
                    value = jnp.concatenate(
                        [
                            acc[second][base + quarter : base + half, :],
                            acc[second][base + half + quarter : base + local, :],
                        ],
                        axis=0,
                    )
                code, scale = coded(value)
                codes1[n][i * half : (i + 1) * half, :] = short(code)
                scale1[n][i : i + 1, :] = scale
            stage1.append(
                exchange(
                    n,
                    codes1,
                    got1,
                    scale1,
                    gots1,
                    (cs1, cr1, ss1, sr1),
                    x_peer if n % 2 == 0 else y_peer,
                )
            )
            if n < WINDOW:
                for copy in stage1[n]:
                    copy.start()

    def middle(n):
        second, first, number = chunks[n]
        for copy in stage1[n]:
            copy.wait_recv()
        for i in range(number):
            base = (first + i) * local
            if n % 2 == 0:
                value = acc[second][base : base + half, :]
            else:
                value = jnp.concatenate(
                    [
                        acc[second][base : base + quarter, :],
                        acc[second][base + half : base + half + quarter, :],
                    ],
                    axis=0,
                )
            value = value + wide(got1[n][i * half : (i + 1) * half, :]) * gots1[n][i : i + 1, :]
            mid[n][i * quarter : (i + 1) * quarter, :] = value[0:quarter]
            code, scale = coded(value[quarter:])
            scale2[n][i : i + 1, :] = scale
            whole2[i * quarter : (i + 1) * quarter, :] = code
        codes2[n][...] = short(whole2[0 : number * quarter, :])
        copies = exchange(
            n,
            codes2,
            got2,
            scale2,
            gots2,
            (cs2, cr2, ss2, sr2),
            y_peer if n % 2 == 0 else x_peer,
        )
        for copy in copies:
            copy.start()
        stage2.append(copies)
        if n + WINDOW < count:
            for copy in stage1[n + WINDOW]:
                copy.start()

    def last(n):
        second, first, number = chunks[n]
        for copy in stage2[n]:
            copy.wait_recv()
        opened = wide(got2[n][...])
        for i in range(number):
            part = slice(i * quarter, (i + 1) * quarter)
            value = mid[n][part, :] + opened[part, :] * gots2[n][i : i + 1, :]
            keep[n][i * own : (i + 1) * own, :] = value[0:own]
            code, scale = coded(value[own:])
            scale3[n][i : i + 1, :] = scale
            for d in range(1, highs):
                whole3[d - 1, i * own : (i + 1) * own, :] = code[(d - 1) * own : d * own]
        copies = []
        for d in range(1, highs):
            codes3[n][d - 1] = short(whole3[d - 1, 0 : number * own, :])
            sem = n * (highs - 1) + d - 1
            copies.append(
                remote(scale3[n], gots3[n].at[d - 1], ss3.at[sem], sr3.at[sem], high_peer(d))
            )
            copies.append(
                remote(
                    codes3[n].at[d - 1], got3[n].at[d - 1], cs3.at[sem], cr3.at[sem], high_peer(d)
                )
            )
        for copy in copies:
            copy.start()
        stage3.append(copies)

    def finish(n, level):
        second, first, number = chunks[n]
        for copy in stage3[n]:
            copy.wait_recv()
        opened = [wide(got3[n][d - 1]) for d in range(1, highs)]
        for i in range(number):
            q = first + i
            value = keep[n][i * own : (i + 1) * own, :]
            for d in range(1, highs):
                value = value + (
                    opened[d - 1][i * own : (i + 1) * own, :] * gots3[n][d - 1, i : i + 1, :]
                )
            factor = 1.0 / (total_cells * jnp.sqrt(level[q : q + 1] * level[second : second + 1]))
            pair = q * terms - q * (q - 1) // 2 + second - q
            out[pair] = value * factor

    level = None
    for t in range(count + 5):
        if t < count:
            middle(t)
        if 0 <= t - 2 < count:
            last(t - 2)
        if t == 3:
            total = gathered(3, level_copies)
            level = jnp.sum(total, axis=1, keepdims=True) / (rows * total_cells) + 1e-06
        if 0 <= t - 5 < count:
            finish(t - 5, level)
    for copies in stage1 + stage2 + stage3:
        sends.extend(copies)
    for copy in sends + across_copies + relays + halos + halo_relays:
        copy.wait_send()


def per_device(basis, slab_region, coef_index, coef_table):
    terms = coef_index.shape[1]
    rows, cells_dev = basis.shape
    slabs_dev = slab_region.shape[0]
    width = cells_dev // slabs_dev
    devices = lax.axis_size("mode")
    highs = devices // 16
    own = rows // devices
    span = slabs_dev * 2
    local = 4 * highs * own
    half, quarter = local // 2, local // 4
    sizes = [number for _, _, number in chunk_list(terms)]
    count = len(sizes)
    tall = terms + -terms % 8
    f32, b16, i16 = jnp.float32, jnp.bfloat16, jnp.int16
    ends = slabs_dev - 2
    depths = [span * width, 2 * ends * width, (span - 2 * ends) * width]
    dma = pltpu.SemaphoreType.DMA
    vmem = pltpu.VMEM
    scratch = [
        vmem((2 * (span + 2), rows, width), b16),
        vmem((4, tall, width), f32),
        vmem((2 * span, tall, width), f32),
        vmem((2 * (span + 2), local, width), b16),
    ]
    scratch += [vmem((terms * local, k), b16) for k in depths]
    scratch += [vmem((2, rows, k), b16) for k in depths]
    scratch += [vmem((CHUNK * quarter, rows), f32), vmem((highs - 1, CHUNK * own, rows), f32)]
    scratch += [vmem(((q + 1) * local, rows), f32) for q in range(terms)]
    for size in (half, quarter):
        scratch += [vmem((n * size, rows), i16) for n in sizes] * 2
        scratch += [vmem((n, rows), f32) for n in sizes] * 2
    scratch += [vmem((highs - 1, n * own, rows), i16) for n in sizes] * 2
    scratch += [vmem((n, rows), f32) for n in sizes]
    scratch += [vmem((highs - 1, n, rows), f32) for n in sizes]
    scratch += [vmem((n * quarter, rows), f32) for n in sizes]
    scratch += [vmem((n * own, rows), f32) for n in sizes]
    fans = (1, 1, 3, highs - 1)
    scratch += [vmem((tall, width), f32)] * 4
    scratch += [vmem((n, tall, width), f32) for n in fans]
    scratch += [dma((slabs_dev,))] * 3
    scratch += [dma((1,))] * 2
    scratch += [dma((slabs_dev,))] * 2
    scratch += [dma((2,))] * 4
    scratch += [dma((3,))] * 2
    scratch += [dma((count,))] * 8
    scratch += [dma((count * (highs - 1),))] * 4
    scratch += [dma((n,)) for n in fans] * 2
    smem = pl.BlockSpec(memory_space=pltpu.SMEM)
    return pl.pallas_call(
        functools.partial(gram_kernel, terms, highs, own, slabs_dev, cells_dev * devices),
        out_shape=jax.ShapeDtypeStruct((terms * (terms + 1) // 2, own, rows), f32),
        in_specs=[pl.BlockSpec(memory_space=pl.ANY), smem, smem, smem],
        out_specs=pl.BlockSpec(memory_space=pltpu.VMEM),
        scratch_shapes=scratch,
        compiler_params=pltpu.CompilerParams(
            collective_id=0, has_side_effects=True, vmem_limit_bytes=62 << 20
        ),
    )(basis, slab_region, coef_index.T, coef_table)


def solution(mesh):
    return jax.shard_map(
        per_device,
        mesh=mesh,
        in_specs=(P("groups", "mode"), P(("groups", "mode")), P("groups", None), P("groups")),
        out_specs=P(None, ("groups", "mode"), None),
        check_vma=False,
    )
```

time: 66.9 us -> 58.4 us (0.87)
  Pallas kernels: 64 us -> 56.3 us
  local copies, waits for them, and re-layouts: 2.69 us -> 1.93 us
    pallas_call x1, Pallas kernels: 64 us -> 56.3 us  [per_device(): pl.pallas_call(functools.partial(gram_kernel, terms, highs, own, slabs_de...]
    unnamed x7 -> x0, local copies, waits for them, and re-layouts: 1.8 us -> none
    pallas_call x1, local copies, waits for them, and re-layouts: 0.89 us -> 1.93 us  [per_device(): pl.pallas_call(functools.partial(gram_kernel, terms, highs, own, slabs_de...]
where the time goes in v2:
time: 58.4 us; the launch traced here: 58.2 us
  Pallas kernels  56.3 us (96%)
  local copies, waits for them, and re-layouts  1.93 us (3%)
    pallas_call x1, Pallas kernels, per_device(): pl.pallas_call(functools.partial(gram_kernel, terms, highs, own, slabs_de...  56.3 us
    pallas_call x1, local copies, waits for them, and re-layouts, per_device(): pl.pallas_call(functools.partial(gram_kernel, terms, highs, own, slabs_de...  1.93 us

profile of v2, /device:TPU:0, one launch (start us, length us, event | category | flops | bytes accessed | tf_op | source)
XLA Modules:
  0.0 58.2 jit_solution(13112274247780269692)
XLA Ops:
  0.0 56.3 %shard_map.46 = f32[21,12,384]{2,1,0:T(8,128)} custom-call(bf16[384,512]{1,0:T(8,128)(2,1)} %refs_0_.1, s32[4]{0:T(128)} %refs_1_.1, s32[6,9]{1,0:T(8,128)} %bitcast.1, f32[8]{0:T(128)} %refs_3_.1), custom_call_target="tpu_custom_call" | custom-call | tf_op jit(solution)/shard_map/pallas_call | solution.py:552
  56.3 1.9 %copy.5 = f32[21,12,384]{2,0,1:T(8,128)} copy(f32[21,12,384]{2,1,0:T(8,128)} %shard_map.46) | data formatting | bytes 774144 | tf_op jit(solution)/shard_map/pallas_call | solution.py:552

commit v3 on v2

--- a/solution.py
+++ b/solution.py
@@ -53,7 +53,7 @@
 
 
 def gram_kernel(terms, highs, own, slabs_dev, total_cells, *refs):
-    basis, region, index, table, out = refs[:5]
+    basis, region_in, index_in, table_in, out = refs[:5]
     chunks = chunk_list(terms)
     count = len(chunks)
     field, packed, weights, mine, lhs1, lhs2, lhs3, act1, act2, act3, whole2, whole3 = refs[5:17]
@@ -66,17 +66,18 @@
         at += count
     (codes1, got1, scale1, gots1, codes2, got2, scale2, gots2) = buffers[:8]
     (codes3, got3, scale3, gots3, mid, keep) = buffers[8:]
-    lvl = refs[at : at + 4]
-    lvl_in = refs[at + 4 : at + 8]
-    at += 8
+    lvl = refs[at : at + 5]
+    lvl_in = refs[at + 5 : at + 10]
+    region, index, table, heard = refs[at + 10 : at + 14]
+    at += 14
     (load_sem, xs, xr, sib_s, sib_r, rel_s, rel_r, hs, hr, hrel_s, hrel_r, ks, kr) = refs[at : at + 13]
     at += 13
     (cs1, cr1, ss1, sr1, cs2, cr2, ss2, sr2, cs3, cr3, ss3, sr3) = refs[at : at + 12]
-    lvl_s = refs[at + 12 : at + 16]
-    lvl_r = refs[at + 16 : at + 20]
+    lvl_s = refs[at + 12 : at + 17]
+    lvl_r = refs[at + 17 : at + 22]
 
     rows, width = field.shape[1], field.shape[2]
-    entries = table.shape[0]
+    entries = table_in.shape[0]
     span = 2 * slabs_dev
     stride = span + 2
     chips = 8 * highs
@@ -106,7 +107,6 @@
     other_behind = across_pair(lax.rem(other + chips - step, chips))
     sibling = chip * 2 + 1 - core
     partner = device(other)
-    cross = other * 2 + 1 - core
     x_peer = device(chip + 1 - 2 * x)
     y_peer = device(chip + 2 - 4 * y)
 
@@ -130,17 +130,25 @@
         )
         for s in range(slabs_dev)
     ]
-    for copy in loads:
+    scalars = [
+        pltpu.make_async_copy(src, dst, load_sem.at[slabs_dev + n])
+        for n, (src, dst) in enumerate(((region_in, region), (index_in, index), (table_in, table)))
+    ]
+    for copy in scalars + loads:
         copy.start()
 
     barrier = pltpu.get_barrier_semaphore()
-    greeted = [sibling, partner, cross, x_peer, y_peer]
-    greeted += [high_peer(d) for d in range(1, highs)]
-    greeted += [device(c) for c in (ahead, behind, other_ahead, other_behind)]
-    for peer in greeted:
+    linked = [partner, x_peer, y_peer] + [high_peer(d) for d in range(1, highs)]
+
+    def signal(semaphore, peer):
         pl.semaphore_signal(
-            barrier, inc=1, device_id={"mode": peer}, device_id_type=pl.DeviceIdType.MESH
-        )
+            semaphore, inc=1, device_id={"mode": peer}, device_id_type=pl.DeviceIdType.MESH
+        )
+
+    for peer in linked + [sibling]:
+        signal(barrier, peer)
+    for copy in scalars:
+        copy.wait()
 
     tall = weights.shape[1]
     piece = width // slabs_dev
@@ -177,7 +185,7 @@
                 source = jnp.where(ri >= place * own, ri + (home * own - place * own), source)
     select = jnp.where(rj == source, 1.0, 0.0).astype(jnp.bfloat16)
 
-    pl.semaphore_wait(barrier, len(greeted))
+    pl.semaphore_wait(barrier, len(linked) + 1)
     for copy in loads:
         copy.wait()
 
@@ -215,15 +223,20 @@
         )
     small = [
         remote(packed.at[core], packed.at[core + shift], ks.at[n], kr.at[n], peer)
-        for n, (peer, shift) in enumerate(((sibling, 0), (partner, 2), (cross, 2)))
+        for n, (peer, shift) in enumerate(((sibling, 0), (partner, 2)))
     ]
-    for copy in small:
+    small.append(remote(packed.at[2 + core], packed.at[2 + core], ks.at[2], kr.at[2], sibling))
+    for copy in small[:2] + across_copies[:1] + [beside] + across_copies[1:]:
         copy.start()
-    across_copies[0].start()
-    halos[0].start()
-    beside.start()
-    for copy in across_copies[1:]:
-        copy.start()
+
+    def tell(n):
+        for peer in linked:
+            signal(heard.at[n], peer)
+
+    def hear(n):
+        pl.semaphore_wait(heard.at[n], len(linked))
+
+    tell(0)
 
     def pick(first, number):
         for s in range(number):
@@ -290,46 +303,57 @@
         return total
 
     ends = slabs_dev - 2
-    part1 = [(0, s) for s in range(span)]
-    part2 = [(1, s) for s in range(span) if s < ends or s >= span - ends]
+    part1 = [(0, s) for s in range(1, span - 1)]
+    part2 = [(0, 0), (0, span - 1)]
+    part2 += [(1, s) for s in range(span) if s < ends or s >= span - ends]
     part3 = [(1, s) for s in range(ends, span - ends)]
     order = list(reversed(range(terms)))
 
-    halos[0].wait_recv()
-    halo_relays[0].start()
+    def expand(first):
+        for n in range(first, first + 2):
+            source_value = packed[n]
+            for s in range(slabs_dev):
+                lanes = (lane_at >= s * piece) & (lane_at < (s + 1) * piece)
+                value = jnp.where(lanes, source_value, 0.0)
+                shift = piece
+                while shift < width:
+                    value = value + pltpu.roll(value, shift, 1)
+                    shift *= 2
+                weights[n * slabs_dev + s] = value
+
+    def pass_on(k):
+        across_copies[k].wait_recv()
+        relays[k].start()
+
+    small[0].wait()
+    expand(0)
+    hear(0)
+    tell(1)
     beside.wait()
-    for copy in small:
-        copy.wait()
-    for n in range(4):
-        source_value = packed[n]
-        for s in range(slabs_dev):
-            lanes = (lane_at >= s * piece) & (lane_at < (s + 1) * piece)
-            value = jnp.where(lanes, source_value, 0.0)
-            shift = piece
-            while shift < width:
-                value = value + pltpu.roll(value, shift, 1)
-                shift *= 2
-            weights[n * slabs_dev + s] = value
-    across_copies[0].wait_recv()
-    relays[0].start()
+    pick(1, span)
+    hear(1)
+    tell(2)
+    small[1].wait()
+    small[2].start()
+    own_actions(lhs1, part1)
+    hear(2)
+    halos[0].start()
+    pass_on(0)
     halos[1].start()
-    halo_relays[0].wait_recv()
-    pick(0, stride)
-    own_actions(lhs1, part1)
     for n, second in enumerate(order):
         all_actions(act1, part1, second)
         acc[second][...] = product(lhs1, act1, second)
-        if n == 0:
-            across_copies[1].wait_recv()
-            relays[1].start()
-        if n == 1:
-            halos[1].wait_recv()
-            halo_relays[1].start()
-        if 2 <= n < slabs_dev - 1 + 0:
-            across_copies[n].wait_recv()
-            relays[n].start()
-    for copy in relays[: slabs_dev - 1] + [halo_relays[1]]:
+        if n < slabs_dev - 2:
+            pass_on(n + 1)
+        if n in (2, 3):
+            halos[n - 2].wait_recv()
+            halo_relays[n - 2].start()
+    small[2].wait()
+    expand(2)
+    for copy in relays[: slabs_dev - 1] + halo_relays:
         copy.wait_recv()
+    pick(0, 1)
+    pick(span + 1, 1)
     pick(stride, ends + 2)
     pick(stride + span - ends, ends + 2)
     own_actions(lhs2, part2)
@@ -337,8 +361,7 @@
         all_actions(act2, part2, second)
         acc[second][...] += product(lhs2, act2, second)
         if n == 2:
-            across_copies[slabs_dev - 1].wait_recv()
-            relays[slabs_dev - 1].start()
+            pass_on(slabs_dev - 1)
     relays[slabs_dev - 1].wait_recv()
     pick(stride + ends + 2, span - 2 * ends - 2)
     own_actions(lhs3, part3)
@@ -355,18 +378,9 @@
             remote(src[n], dst[n], cs.at[n], cr.at[n], peer),
         ]
 
-    for turn_at, second in enumerate(order):
+    for second in order:
         all_actions(act3, part3, second)
         acc[second][...] += product(lhs3, act3, second)
-        if turn_at == 0:
-            lvl[1][...] = gathered(0, level_copies)
-            level_copies = spread(1, [y_peer])
-        if turn_at == 2:
-            lvl[2][...] = gathered(1, level_copies)
-            level_copies = spread(2, [sibling, partner, cross])
-        if turn_at == 4:
-            lvl[3][...] = gathered(2, level_copies)
-            level_copies = spread(3, [high_peer(d) for d in range(1, highs)])
         for n, (chunk_second, first, number) in enumerate(chunks):
             if chunk_second != second:
                 continue
@@ -484,16 +498,30 @@
             out[pair] = value * factor
 
     level = None
-    for t in range(count + 5):
+    finished = 0
+    for t in range(count + 8):
         if t < count:
             middle(t)
-        if 0 <= t - 2 < count:
-            last(t - 2)
-        if t == 3:
-            total = gathered(3, level_copies)
+        if t == 0:
+            lvl[1][...] = gathered(0, level_copies)
+            level_copies = spread(1, [y_peer])
+        if 0 <= t - 4 < count:
+            last(t - 4)
+        if t == 4:
+            lvl[2][...] = gathered(1, level_copies)
+            level_copies = spread(2, [high_peer(d) for d in range(1, highs)])
+        if t == 7:
+            lvl[3][...] = gathered(2, level_copies)
+            level_copies = spread(3, [partner])
+        if t == 8:
+            lvl[4][...] = gathered(3, level_copies)
+            level_copies = spread(4, [sibling])
+        if t == 10:
+            total = gathered(4, level_copies)
             level = jnp.sum(total, axis=1, keepdims=True) / (rows * total_cells) + 1e-06
-        if 0 <= t - 5 < count:
-            finish(t - 5, level)
+        while t >= 10 and finished <= t - 8 and finished < count:
+            finish(finished, level)
+            finished += 1
     for copies in stage1 + stage2 + stage3:
         sends.extend(copies)
     for copy in sends + across_copies + relays + halos + halo_relays:
@@ -516,7 +544,7 @@
     tall = terms + -terms % 8
     f32, b16, i16 = jnp.float32, jnp.bfloat16, jnp.int16
     ends = slabs_dev - 2
-    depths = [span * width, 2 * ends * width, (span - 2 * ends) * width]
+    depths = [(span - 2) * width, (2 * ends + 2) * width, (span - 2 * ends) * width]
     dma = pltpu.SemaphoreType.DMA
     vmem = pltpu.VMEM
     scratch = [
@@ -537,10 +565,17 @@
     scratch += [vmem((highs - 1, n, rows), f32) for n in sizes]
     scratch += [vmem((n * quarter, rows), f32) for n in sizes]
     scratch += [vmem((n * own, rows), f32) for n in sizes]
-    fans = (1, 1, 3, highs - 1)
-    scratch += [vmem((tall, width), f32)] * 4
+    fans = (1, 1, highs - 1, 1, 1)
+    scratch += [vmem((tall, width), f32)] * 5
     scratch += [vmem((n, tall, width), f32) for n in fans]
-    scratch += [dma((slabs_dev,))] * 3
+    scratch += [
+        pltpu.SMEM(slab_region.shape, jnp.int32),
+        pltpu.SMEM(coef_index.shape[::-1], jnp.int32),
+        pltpu.SMEM(coef_table.shape, f32),
+        pltpu.SemaphoreType.REGULAR((3,)),
+        dma((slabs_dev + 3,)),
+    ]
+    scratch += [dma((slabs_dev,))] * 2
     scratch += [dma((1,))] * 2
     scratch += [dma((slabs_dev,))] * 2
     scratch += [dma((2,))] * 4
@@ -548,11 +583,10 @@
     scratch += [dma((count,))] * 8
     scratch += [dma((count * (highs - 1),))] * 4
     scratch += [dma((n,)) for n in fans] * 2
-    smem = pl.BlockSpec(memory_space=pltpu.SMEM)
     return pl.pallas_call(
         functools.partial(gram_kernel, terms, highs, own, slabs_dev, cells_dev * devices),
         out_shape=jax.ShapeDtypeStruct((terms * (terms + 1) // 2, own, rows), f32),
-        in_specs=[pl.BlockSpec(memory_space=pl.ANY), smem, smem, smem],
+        in_specs=[pl.BlockSpec(memory_space=pltpu.HBM)] * 4,
         out_specs=pl.BlockSpec(memory_space=pltpu.VMEM),
         scratch_shapes=scratch,
         compiler_params=pltpu.CompilerParams(

time: 58.4 us -> 51 us (0.87)
  Pallas kernels: 56.3 us -> 48.8 us
    pallas_call x1, Pallas kernels: 56.3 us -> 48.8 us  [per_device(): pl.pallas_call(functools.partial(gram_kernel, terms, highs, own, slabs_de...]
where the time goes in v3:
time: 51 us; the launch traced here: 50.8 us
  Pallas kernels  48.8 us (96%)
  local copies, waits for them, and re-layouts  1.93 us (4%)
    pallas_call x1, Pallas kernels, per_device(): pl.pallas_call(functools.partial(gram_kernel, terms, highs, own, slabs_de...  48.8 us
    pallas_call x1, local copies, waits for them, and re-layouts, per_device(): pl.pallas_call(functools.partial(gram_kernel, terms, highs, own, slabs_de...  1.93 us

profile of v3, /device:TPU:0, one launch (start us, length us, event | category | flops | bytes accessed | tf_op | source)
XLA Modules:
  0.0 50.8 jit_solution(11017008473607685561)
XLA Ops:
  0.0 48.8 %shard_map.46 = f32[21,12,384]{2,1,0:T(8,128)} custom-call(bf16[384,512]{1,0:T(8,128)(2,1)} %refs_0_.1, s32[4]{0:T(128)} %refs_1_.1, s32[6,9]{1,0:T(8,128)} %bitcast.1, f32[8]{0:T(128)} %refs_3_.1), custom_call_target="tpu_custom_call" | custom-call | tf_op jit(solution)/shard_map/pallas_call | solution.py:586
  48.8 1.9 %copy.5 = f32[21,12,384]{2,0,1:T(8,128)} copy(f32[21,12,384]{2,1,0:T(8,128)} %shard_map.46) | data formatting | bytes 774144 | tf_op jit(solution)/shard_map/pallas_call | solution.py:586

commit v4 on v3

--- a/solution.py
+++ b/solution.py
@@ -9,11 +9,13 @@
 
 CHUNK = 2
 WINDOW = 4
+EARLY = 0
+LAG = 4
 
 
 def chunk_list(terms):
     chunks = []
-    for second in reversed(range(terms)):
+    for second in range(terms):
         first = 0
         while first <= second:
             number = min(CHUNK, second + 1 - first)
@@ -102,9 +104,7 @@
     other = across_pair(chip)
     step = 2 * core - 1
     ahead = lax.rem(chip + chips + step, chips)
-    behind = lax.rem(chip + chips - step, chips)
-    other_ahead = across_pair(lax.rem(other + chips + step, chips))
-    other_behind = across_pair(lax.rem(other + chips - step, chips))
+    other_next = lax.rem(other + chips + step, chips)
     sibling = chip * 2 + 1 - core
     partner = device(other)
     x_peer = device(chip + 1 - 2 * x)
@@ -207,17 +207,22 @@
     beyond = (1 - core) * (span + 1)
     halos = []
     halo_relays = []
-    for n, target in enumerate((ahead, other_ahead)):
+    arrivals = []
+    for n, (origin, toward) in enumerate(((chip, ahead), (other, other_next))):
+        inside = jnp.where((toward // 4) == (origin // 4) + 1 - 2 * ((origin // 4) % 2), 1, 0)
+        landing = n + inside - 2 * n * inside
+        target = toward + landing * (across_pair(toward) - toward)
         halos.append(
             remote(
                 field.at[n * stride + edge],
-                field.at[n * stride + beyond],
+                field.at[landing * stride + beyond],
                 hs.at[n],
-                hr.at[n],
+                hr.at[landing],
                 device(target),
             )
         )
         slot = n * stride + beyond
+        arrivals.append(remote(field.at[slot], field.at[slot], hs.at[n], hr.at[n], partner))
         halo_relays.append(
             remote(field.at[slot], field.at[slot], hrel_s.at[n], hrel_r.at[n], sibling)
         )
@@ -260,15 +265,14 @@
 
     lvl[0][...] = jnp.zeros_like(lvl[0])
 
-    def own_actions(lhs, part):
-        for term in range(terms):
-            squares = None
-            for s, spot in enumerate(part):
-                value = acted(term, mine, spot)
-                lhs[term * local : (term + 1) * local, s * width : (s + 1) * width] = value
-                value = value.astype(jnp.float32)
-                squares = value * value if squares is None else squares + value * value
-            lvl[0][term : term + 1, :] += jnp.sum(squares, axis=0, keepdims=True)
+    def own_action(lhs, part, term):
+        squares = None
+        for s, spot in enumerate(part):
+            value = acted(term, mine, spot)
+            lhs[term * local : (term + 1) * local, s * width : (s + 1) * width] = value
+            value = value.astype(jnp.float32)
+            squares = value * value if squares is None else squares + value * value
+        lvl[0][term : term + 1, :] += jnp.sum(squares, axis=0, keepdims=True)
 
     def all_actions(act, part, second):
         for s, spot in enumerate(part):
@@ -304,10 +308,10 @@
 
     ends = slabs_dev - 2
     part1 = [(0, s) for s in range(1, span - 1)]
-    part2 = [(0, 0), (0, span - 1)]
-    part2 += [(1, s) for s in range(span) if s < ends or s >= span - ends]
+    part2 = [(1, s) for s in range(1, span - 1) if s < ends or s >= span - ends]
     part3 = [(1, s) for s in range(ends, span - ends)]
-    order = list(reversed(range(terms)))
+    part3 += [(n, s) for n in range(2) for s in (0, span - 1)]
+    order = list(range(terms))
 
     def expand(first):
         for n in range(first, first + 2):
@@ -335,37 +339,40 @@
     tell(2)
     small[1].wait()
     small[2].start()
-    own_actions(lhs1, part1)
     hear(2)
     halos[0].start()
     pass_on(0)
     halos[1].start()
-    for n, second in enumerate(order):
+    for second in order:
+        own_action(lhs1, part1, second)
         all_actions(act1, part1, second)
         acc[second][...] = product(lhs1, act1, second)
-        if n < slabs_dev - 2:
-            pass_on(n + 1)
-        if n in (2, 3):
-            halos[n - 2].wait_recv()
-            halo_relays[n - 2].start()
+        if second == 2:
+            pass_on(1)
     small[2].wait()
     expand(2)
-    for copy in relays[: slabs_dev - 1] + halo_relays:
+    pass_on(2)
+    for copy in relays[: slabs_dev - 1]:
         copy.wait_recv()
-    pick(0, 1)
-    pick(span + 1, 1)
-    pick(stride, ends + 2)
-    pick(stride + span - ends, ends + 2)
-    own_actions(lhs2, part2)
-    for n, second in enumerate(order):
+    pick(stride + 1, ends + 1)
+    pick(stride + span - ends, ends + 1)
+    for second in order:
+        own_action(lhs2, part2, second)
         all_actions(act2, part2, second)
         acc[second][...] += product(lhs2, act2, second)
-        if n == 2:
+        if second == 0:
+            for n in range(2):
+                arrivals[n].wait_recv()
+                halo_relays[n].start()
+        if second == 2:
             pass_on(slabs_dev - 1)
+    for copy in halo_relays:
+        copy.wait_recv()
+    for n in range(2):
+        pick(n * stride, 1)
+        pick(n * stride + span + 1, 1)
     relays[slabs_dev - 1].wait_recv()
     pick(stride + ends + 2, span - 2 * ends - 2)
-    own_actions(lhs3, part3)
-    level_copies = spread(0, [x_peer])
 
     stage1 = []
     stage2 = []
@@ -378,7 +385,54 @@
             remote(src[n], dst[n], cs.at[n], cr.at[n], peer),
         ]
 
+    progress = {"middle": 0, "started": 0}
+
+    def pump():
+        while progress["started"] < min(len(stage1), progress["middle"] + WINDOW):
+            for copy in stage1[progress["started"]]:
+                copy.start()
+            progress["started"] += 1
+
+    def middle(n):
+        second, first, number = chunks[n]
+        for copy in stage1[n]:
+            copy.wait_recv()
+        for i in range(number):
+            base = (first + i) * local
+            if n % 2 == 0:
+                value = acc[second][base : base + half, :]
+            else:
+                value = jnp.concatenate(
+                    [
+                        acc[second][base : base + quarter, :],
+                        acc[second][base + half : base + half + quarter, :],
+                    ],
+                    axis=0,
+                )
+            value = value + wide(got1[n][i * half : (i + 1) * half, :]) * gots1[n][i : i + 1, :]
+            mid[n][i * quarter : (i + 1) * quarter, :] = value[0:quarter]
+            code, scale = coded(value[quarter:])
+            scale2[n][i : i + 1, :] = scale
+            whole2[i * quarter : (i + 1) * quarter, :] = code
+        codes2[n][...] = short(whole2[0 : number * quarter, :])
+        copies = exchange(
+            n,
+            codes2,
+            got2,
+            scale2,
+            gots2,
+            (cs2, cr2, ss2, sr2),
+            y_peer if n % 2 == 0 else x_peer,
+        )
+        for copy in copies:
+            copy.start()
+        stage2.append(copies)
+        progress["middle"] += 1
+        pump()
+
     for second in order:
+        if second == 0:
+            own_action(lhs3, part3, 0)
         all_actions(act3, part3, second)
         acc[second][...] += product(lhs3, act3, second)
         for n, (chunk_second, first, number) in enumerate(chunks):
@@ -410,47 +464,13 @@
                     x_peer if n % 2 == 0 else y_peer,
                 )
             )
-            if n < WINDOW:
-                for copy in stage1[n]:
-                    copy.start()
-
-    def middle(n):
-        second, first, number = chunks[n]
-        for copy in stage1[n]:
-            copy.wait_recv()
-        for i in range(number):
-            base = (first + i) * local
-            if n % 2 == 0:
-                value = acc[second][base : base + half, :]
-            else:
-                value = jnp.concatenate(
-                    [
-                        acc[second][base : base + quarter, :],
-                        acc[second][base + half : base + half + quarter, :],
-                    ],
-                    axis=0,
-                )
-            value = value + wide(got1[n][i * half : (i + 1) * half, :]) * gots1[n][i : i + 1, :]
-            mid[n][i * quarter : (i + 1) * quarter, :] = value[0:quarter]
-            code, scale = coded(value[quarter:])
-            scale2[n][i : i + 1, :] = scale
-            whole2[i * quarter : (i + 1) * quarter, :] = code
-        codes2[n][...] = short(whole2[0 : number * quarter, :])
-        copies = exchange(
-            n,
-            codes2,
-            got2,
-            scale2,
-            gots2,
-            (cs2, cr2, ss2, sr2),
-            y_peer if n % 2 == 0 else x_peer,
-        )
-        for copy in copies:
-            copy.start()
-        stage2.append(copies)
-        if n + WINDOW < count:
-            for copy in stage1[n + WINDOW]:
-                copy.start()
+        pump()
+        if second == 0:
+            for term in order[1:]:
+                own_action(lhs3, part3, term)
+            hops = spread(0, [x_peer])
+        while progress["middle"] < EARLY + second - terms + 1:
+            middle(progress["middle"])
 
     def last(n):
         second, first, number = chunks[n]
@@ -499,27 +519,27 @@
 
     level = None
     finished = 0
-    for t in range(count + 8):
-        if t < count:
+    for t in range(count + LAG + 4):
+        if progress["middle"] <= t < count:
             middle(t)
-        if t == 0:
-            lvl[1][...] = gathered(0, level_copies)
-            level_copies = spread(1, [y_peer])
-        if 0 <= t - 4 < count:
-            last(t - 4)
-        if t == 4:
-            lvl[2][...] = gathered(1, level_copies)
-            level_copies = spread(2, [high_peer(d) for d in range(1, highs)])
-        if t == 7:
-            lvl[3][...] = gathered(2, level_copies)
-            level_copies = spread(3, [partner])
-        if t == 8:
-            lvl[4][...] = gathered(3, level_copies)
-            level_copies = spread(4, [sibling])
-        if t == 10:
-            total = gathered(4, level_copies)
+        if t == 1:
+            lvl[1][...] = gathered(0, hops)
+            hops = spread(1, [y_peer])
+        if 0 <= t - LAG < count:
+            last(t - LAG)
+        if t == LAG:
+            lvl[2][...] = gathered(1, hops)
+            hops = spread(2, [high_peer(d) for d in range(1, highs)])
+        if t == LAG + 2:
+            lvl[3][...] = gathered(2, hops)
+            hops = spread(3, [partner])
+        if t == LAG + 4:
+            lvl[4][...] = gathered(3, hops)
+            hops = spread(4, [sibling])
+        if t == LAG + 6:
+            total = gathered(4, hops)
             level = jnp.sum(total, axis=1, keepdims=True) / (rows * total_cells) + 1e-06
-        while t >= 10 and finished <= t - 8 and finished < count:
+        while t >= LAG + 6 and finished <= t - LAG - 4 and finished < count:
             finish(finished, level)
             finished += 1
     for copies in stage1 + stage2 + stage3:
@@ -544,7 +564,7 @@
     tall = terms + -terms % 8
     f32, b16, i16 = jnp.float32, jnp.bfloat16, jnp.int16
     ends = slabs_dev - 2
-    depths = [(span - 2) * width, (2 * ends + 2) * width, (span - 2 * ends) * width]
+    depths = [(span - 2) * width, 2 * (ends - 1) * width, (span - 2 * ends + 4) * width]
     dma = pltpu.SemaphoreType.DMA
     vmem = pltpu.VMEM
     scratch = [

time: 51 us -> 47.6 us (0.933)
  Pallas kernels: 48.8 us -> 45.5 us
    pallas_call x1, Pallas kernels: 48.8 us -> 45.5 us  [per_device(): pl.pallas_call(functools.partial(gram_kernel, terms, highs, own, slabs_de...]
where the time goes in v4:
time: 47.6 us; the launch traced here: 47.5 us
  Pallas kernels  45.5 us (96%)
  local copies, waits for them, and re-layouts  1.93 us (4%)
    pallas_call x1, Pallas kernels, per_device(): pl.pallas_call(functools.partial(gram_kernel, terms, highs, own, slabs_de...  45.5 us
    pallas_call x1, local copies, waits for them, and re-layouts, per_device(): pl.pallas_call(functools.partial(gram_kernel, terms, highs, own, slabs_de...  1.93 us

profile of v4, /device:TPU:0, one launch (start us, length us, event | category | flops | bytes accessed | tf_op | source)
XLA Modules:
  0.0 47.5 jit_solution(13254017920462855117)
XLA Ops:
  0.0 45.5 %shard_map.46 = f32[21,12,384]{2,1,0:T(8,128)} custom-call(bf16[384,512]{1,0:T(8,128)(2,1)} %refs_0_.1, s32[4]{0:T(128)} %refs_1_.1, s32[6,9]{1,0:T(8,128)} %bitcast.1, f32[8]{0:T(128)} %refs_3_.1), custom_call_target="tpu_custom_call" | custom-call | tf_op jit(solution)/shard_map/pallas_call | solution.py:606
  45.5 1.9 %copy.5 = f32[21,12,384]{2,0,1:T(8,128)} copy(f32[21,12,384]{2,1,0:T(8,128)} %shard_map.46) | data formatting | bytes 774144 | tf_op jit(solution)/shard_map/pallas_call | solution.py:606

commit v5 on v4

--- a/solution.py
+++ b/solution.py
@@ -7,10 +7,10 @@
 from jax.experimental.pallas import tpu as pltpu
 from jax.sharding import PartitionSpec as P
 
-CHUNK = 2
+CHUNK = 3
 WINDOW = 4
 EARLY = 0
-LAG = 4
+LAG = 3
 
 
 def chunk_list(terms):
@@ -18,7 +18,7 @@
     for second in range(terms):
         first = 0
         while first <= second:
-            number = min(CHUNK, second + 1 - first)
+            number = -(-(second + 1 - first) // -(-(second + 1 - first) // CHUNK))
             chunks.append((second, first, number))
             first += number
     return chunks
@@ -231,7 +231,7 @@
         for n, (peer, shift) in enumerate(((sibling, 0), (partner, 2)))
     ]
     small.append(remote(packed.at[2 + core], packed.at[2 + core], ks.at[2], kr.at[2], sibling))
-    for copy in small[:2] + across_copies[:1] + [beside] + across_copies[1:]:
+    for copy in small[:2] + across_copies[:1] + [beside] + across_copies[1:-1]:
         copy.start()
 
     def tell(n):
@@ -343,6 +343,7 @@
     halos[0].start()
     pass_on(0)
     halos[1].start()
+    across_copies[slabs_dev - 1].start()
     for second in order:
         own_action(lhs1, part1, second)
         all_actions(act1, part1, second)
@@ -352,6 +353,9 @@
     small[2].wait()
     expand(2)
     pass_on(2)
+    for n in range(2):
+        arrivals[n].wait_recv()
+        halo_relays[n].start()
     for copy in relays[: slabs_dev - 1]:
         copy.wait_recv()
     pick(stride + 1, ends + 1)
@@ -360,10 +364,6 @@
         own_action(lhs2, part2, second)
         all_actions(act2, part2, second)
         acc[second][...] += product(lhs2, act2, second)
-        if second == 0:
-            for n in range(2):
-                arrivals[n].wait_recv()
-                halo_relays[n].start()
         if second == 2:
             pass_on(slabs_dev - 1)
     for copy in halo_relays:
@@ -610,9 +610,14 @@
         out_specs=pl.BlockSpec(memory_space=pltpu.VMEM),
         scratch_shapes=scratch,
         compiler_params=pltpu.CompilerParams(
-            collective_id=0, has_side_effects=True, vmem_limit_bytes=62 << 20
+            collective_id=0, has_side_effects=True, vmem_limit_bytes=40 << 20
         ),
-    )(basis, slab_region, coef_index.T, coef_table)
+    )(
+        pltpu.with_memory_space_constraint(basis, pltpu.HBM),
+        pltpu.with_memory_space_constraint(slab_region, pltpu.HBM),
+        pltpu.with_memory_space_constraint(coef_index.T, pltpu.HBM),
+        pltpu.with_memory_space_constraint(coef_table, pltpu.HBM),
+    )
 
 
 def solution(mesh):

time: 47.6 us -> 43.9 us (0.922)
  Pallas kernels: 45.5 us -> 42.8 us
  local copies, waits for them, and re-layouts: 1.93 us -> 0.89 us
    pallas_call x1, Pallas kernels: 45.5 us -> 42.8 us  [per_device(): pl.pallas_call(functools.partial(gram_kernel, terms, highs, own, slabs_de...]
    pallas_call x1, local copies, waits for them, and re-layouts: 1.93 us -> 0.89 us  [per_device(): pl.pallas_call(functools.partial(gram_kernel, terms, highs, own, slabs_de...]
where the time goes in v5:
time: 43.9 us; the launch traced here: 43.7 us
  Pallas kernels  42.8 us (97%)
  local copies, waits for them, and re-layouts  0.89 us (2%)
    pallas_call x1, Pallas kernels, per_device(): pl.pallas_call(functools.partial(gram_kernel, terms, highs, own, slabs_de...  42.8 us
    pallas_call x1, local copies, waits for them, and re-layouts, per_device(): pl.pallas_call(functools.partial(gram_kernel, terms, highs, own, slabs_de...  0.89 us

profile of v5, /device:TPU:0, one launch (start us, length us, event | category | flops | bytes accessed | tf_op | source)
XLA Modules:
  0.0 43.7 jit_solution(18295798522221489518)
XLA Ops:
  0.0 42.8 %shard_map.46 = f32[21,12,384]{2,1,0:T(8,128)S(1)} custom-call(bf16[384,512]{1,0:T(8,128)(2,1)} %refs_0_.1, s32[4]{0:T(128)} %refs_1_.1, s32[6,9]{1,0:T(8,128)} %bitcast.1, f32[8]{0:T(128)} %refs_3_.1), custom_call_target="tpu_custom_call" | custom-call | tf_op jit(solution)/shard_map/pallas_call | solution.py:606
  42.8 0.9 %copy.5 = f32[21,12,384]{2,0,1:T(8,128)} copy(f32[21,12,384]{2,1,0:T(8,128)S(1)} %shard_map.46) | data formatting | bytes 774144 | tf_op jit(solution)/shard_map/pallas_call | solution.py:606

commit v6 on v5

--- a/solution.py
+++ b/solution.py
@@ -431,8 +431,8 @@
         pump()
 
     for second in order:
-        if second == 0:
-            own_action(lhs3, part3, 0)
+        if second < 2:
+            own_action(lhs3, part3, second)
         all_actions(act3, part3, second)
         acc[second][...] += product(lhs3, act3, second)
         for n, (chunk_second, first, number) in enumerate(chunks):
@@ -465,8 +465,8 @@
                 )
             )
         pump()
-        if second == 0:
-            for term in order[1:]:
+        if second == 1:
+            for term in order[2:]:
                 own_action(lhs3, part3, term)
             hops = spread(0, [x_peer])
         while progress["middle"] < EARLY + second - terms + 1:

time: 43.9 us -> 43.7 us (level)
  no operation moved by 1% of the time
where the time goes in v6:
time: 43.7 us; the launch traced here: 43.5 us
  Pallas kernels  42.6 us (97%)
  local copies, waits for them, and re-layouts  0.89 us (2%)
    pallas_call x1, Pallas kernels, per_device(): pl.pallas_call(functools.partial(gram_kernel, terms, highs, own, slabs_de...  42.6 us
    pallas_call x1, local copies, waits for them, and re-layouts, per_device(): pl.pallas_call(functools.partial(gram_kernel, terms, highs, own, slabs_de...  0.89 us

profile of v6, /device:TPU:0, one launch (start us, length us, event | category | flops | bytes accessed | tf_op | source)
XLA Modules:
  0.0 43.5 jit_solution(5155951547869084499)
XLA Ops:
  0.0 42.6 %shard_map.46 = f32[21,12,384]{2,1,0:T(8,128)S(1)} custom-call(bf16[384,512]{1,0:T(8,128)(2,1)} %refs_0_.1, s32[4]{0:T(128)} %refs_1_.1, s32[6,9]{1,0:T(8,128)} %bitcast.1, f32[8]{0:T(128)} %refs_3_.1), custom_call_target="tpu_custom_call" | custom-call | tf_op jit(solution)/shard_map/pallas_call | solution.py:606
  42.7 0.9 %copy.5 = f32[21,12,384]{2,0,1:T(8,128)} copy(f32[21,12,384]{2,1,0:T(8,128)S(1)} %shard_map.46) | data formatting | bytes 774144 | tf_op jit(solution)/shard_map/pallas_call | solution.py:606
